TPU v7x, 128 devices: a whole 4x4x4 slice. The times are simulated.
128 devices in a mesh: mem: 8 (over z, core), grid: 16 (over x, y).
Axes of the slice: x: 4, y: 4, z: 4, core: 2. Of those that a mesh axis runs over, the one named last changes fastest.
Arguments:
- state: float32 [80, 524288], P('mem', 'grid'), may hold values from -6 to 6
- obs_tile: int32 [4], replicated, may hold values from 0 to 4095
- obs_offset: int32 [4, 256], replicated, may hold values from 0 to 127
- obs_value: float32 [4, 256], replicated, may hold values from -8 to 8
- obs_error: float32 [4, 256], replicated, may hold values from 0.5 to 4
- loc_mask: int32 [4, 4096], replicated, may hold values 0 or 1
- block_order: int32 [4], replicated, may hold values from 0 to 3, each once
Outputs:
- posterior: float32 [80, 524288], P('mem', 'grid')
Inputs may be any that keep to these rules, and one draw needn't show every extreme that they name: `block_order`: a permutation of 0 to 3.
All inputs are finite; a program needn't handle non-finite values.
Results may differ from a plain program's by a relative error of at most 0.00024.
Values sent between devices are 32-bit elements; how exact they have to be, the bound alone decides.
A program may use at most 64 MiB of HBM per device.

v0:
```python
import jax
import jax.numpy as jnp
from jax import lax
from jax.sharding import PartitionSpec as P

BLOCKS = 4
TILE = 128


def from_root(value, axis, root):
    mine = lax.axis_index(axis) == root
    return lax.psum(jnp.where(mine, value, jnp.zeros_like(value)), axis)


def on_device(state, obs_tile, obs_offset, obs_value, obs_error, loc_mask, block_order):
    highest = lax.Precision.HIGHEST
    n_mem = lax.axis_size("mem")
    n_grid = lax.axis_size("grid")
    mem_idx = lax.axis_index("mem")
    grid_idx = lax.axis_index("grid")
    my_rank = mem_idx * n_grid + grid_idx
    mem_loc = state.shape[0]
    grid_width = state.shape[1]
    members = mem_loc * n_mem
    piece = grid_width // (n_mem * n_grid)
    moved = lax.all_to_all(state, ("mem", "grid"), split_axis=1, concat_axis=0, tiled=True)
    field = moved.reshape(n_mem, n_grid, mem_loc, piece)
    n_part = field.shape[1]
    for k in range(BLOCKS):
        b = block_order[k]
        base = obs_tile[b] * TILE
        owner_grid = base // grid_width
        rest = base % grid_width
        root = rest // piece
        masks = loc_mask[b].reshape(n_grid, n_mem * n_grid, piece // TILE)
        local_mask = lax.dynamic_slice_in_dim(masks, my_rank, 1, 1)[:, 0, :]
        col = rest % piece
        zero = jnp.zeros((), jnp.int32)
        slab = lax.dynamic_slice(field, (zero, owner_grid, zero, col), (n_mem, 1, mem_loc, TILE))
        slab = slab.reshape(members, TILE)
        local_prior = jnp.take(slab, obs_offset[b], axis=1)
        prior = from_root(local_prior, ("mem", "grid"), root)
        ybar = jnp.mean(prior, axis=0)
        dev = prior - ybar
        var = jnp.sum(dev * dev, axis=0) / (members - 1.0)
        error = obs_error[b]
        dy_inc = (
            var / (var + error) * (obs_value[b] - ybar)
            + (jnp.sqrt(error / (var + error)) - 1.0) * dev
        )
        weighted = dev / ((members - 1.0) * (var + 1e-05))
        weighted = weighted.reshape(n_mem, mem_loc, -1)
        dy_inc = dy_inc.reshape(n_mem, mem_loc, -1)
        anom = field - jnp.mean(field, axis=(0, 2), keepdims=True)
        coef = jnp.einsum("agmp,amo->gpo", anom, weighted, precision=highest)
        incr = jnp.einsum("gpo,amo->agmp", coef, dy_inc, precision=highest)
        spread = jnp.broadcast_to(
            local_mask.astype(jnp.float32)[:, :, None], (n_part, piece // TILE, TILE)
        ).reshape(n_part, piece)
        field = field + incr * spread[None, :, None, :]
    flat = field.reshape(n_mem * n_grid * mem_loc, piece)
    return lax.all_to_all(flat, ("mem", "grid"), split_axis=0, concat_axis=1, tiled=True)


def solution(mesh):
    placed = (P("mem", "grid"), P(), P(), P(), P(), P(), P())
    return jax.shard_map(
        on_device, mesh=mesh, in_specs=placed, out_specs=P("mem", "grid"), check_vma=False
    )
```

profile of v0, /device:TPU:1, one launch (start us, length us, event | category | flops | bytes accessed | tf_op | source)
XLA Modules:
  0.0 693.8 jit_solution(1083776546542373088)
XLA Ops:
  6.5 2.2 copy.92
  8.8 0.1 slice.24
  8.8 2.1 copy.62
  11.0 11.5 %all-to-all-start = ((f32[10,128,256]{2,0,1:T(8,128)}), f32[10,128,256]{2,0,1:T(8,128)S(1)}, u32[]{:S(2)}, u32[]{:S(2)}) async-start(f32[10,128,256]{2,0,1:T(8,128)} %copy.62), calls=%async_computation | async-start | bytes 4194304 | tf_op jit(solution)/shard_map/all_to_all | solution.py:26
  22.5 0.7 fusion.27
  30.8 0.7 fusion.26
  34.2 0.2 dynamic-slice_reduce_fusion
  34.4 1.0 reshape_squeeze.12
  35.5 0.1 copy.66
  35.7 1.0 reshape_squeeze.13
  36.8 0.1 copy.70
  37.0 1.0 reshape_squeeze.14
  38.1 0.1 copy.74
  38.3 1.0 reshape_squeeze.15
  39.5 0.1 copy.78
  39.8 12.4 %all-to-all-done = f32[10,128,256]{2,0,1:T(8,128)S(1)} async-done(((f32[10,128,256]{2,0,1:T(8,128)}), f32[10,128,256]{2,0,1:T(8,128)S(1)}, u32[]{:S(2)}, u32[]{:S(2)}) %all-to-all-start) | async-done | bytes 1310752 | tf_op jit(solution)/shard_map/all_to_all | solution.py:26
  52.3 0.1 copy.63
  52.4 0.7 gather_fusion
  53.3 0.6 bitcast_select_fusion.3
  53.9 0.6 all-reduce.7.cloned.1.call-start
  54.5 0.4 bitcast_reduce_fusion
  54.9 1.7 bitcast_subtract_fusion
  56.6 132.0 %all-reduce.5.cloned.1.call-done = f32[80,256]{1,0:T(8,128)} async-done(((f32[80,256]{1,0:T(8,128)}), f32[80,256]{1,0:T(8,128)}) %all-reduce.5.cloned.1.call-update) | async-done | bytes 81936 | tf_op jit(solution)/shard_map/psum | solution.py:12
  188.6 0.9 reduce_sum.115
  189.5 0.9 multiply_reduce_fusion.3
  190.5 0.9 multiply_add_fusion.3
  191.5 5.1 fusion.15
  196.6 4.4 fusion.28
  201.0 1.3 copy-done
  202.4 0.1 copy.67
  202.5 0.7 gather_fusion.1
  203.3 0.6 bitcast_select_fusion.2
  204.0 0.2 all-reduce.9.cloned.1.call-start
  204.2 135.2 %all-reduce.7.cloned.1.call-done = f32[80,256]{1,0:T(8,128)} async-done(((f32[80,256]{1,0:T(8,128)}), f32[80,256]{1,0:T(8,128)}) %all-reduce.7.cloned.1.call-update) | async-done | bytes 81936 | tf_op jit(solution)/shard_map/psum | solution.py:12
  339.4 0.9 reduce_sum.120
  340.3 0.9 multiply_reduce_fusion.2
  341.3 0.9 multiply_add_fusion.2
  342.2 3.5 fusion.4
  345.8 4.4 fusion.29
  350.2 1.3 copy-done.2
  351.6 0.1 copy.71
  351.7 0.7 gather_fusion.2
  352.6 0.6 bitcast_select_fusion.1
  353.2 0.3 all-reduce.11.cloned.1.call-start
  353.5 135.1 %all-reduce.9.cloned.1.call-done = f32[80,256]{1,0:T(8,128)} async-done(((f32[80,256]{1,0:T(8,128)}), f32[80,256]{1,0:T(8,128)}) %all-reduce.9.cloned.1.call-update) | async-done | bytes 81936 | tf_op jit(solution)/shard_map/psum | solution.py:12
  488.6 0.9 reduce_sum.123
  489.5 0.9 multiply_reduce_fusion.1
  490.4 0.9 multiply_add_fusion.1
  491.4 3.5 fusion.2
  494.9 4.4 fusion.30
  499.4 1.3 copy-done.4
  500.8 0.1 copy.75
  500.9 0.7 gather_fusion.3
  501.7 0.6 bitcast_select_fusion
  502.4 135.4 %all-reduce.11.cloned.1.call-done = f32[80,256]{1,0:T(8,128)} async-done(((f32[80,256]{1,0:T(8,128)}), f32[80,256]{1,0:T(8,128)}) %all-reduce.11.cloned.1.call-update) | async-done | bytes 81936 | tf_op jit(solution)/shard_map/psum | solution.py:12
  637.8 0.9 reduce_sum.126
  638.7 0.9 multiply_reduce_fusion
  639.6 0.9 multiply_add_fusion
  640.6 3.5 fusion
  644.2 4.7 bitcast_add_fusion
  648.8 34.7 %all_to_all.35 = f32[128,10,256]{2,1,0:T(8,128)S(1)} all-to-all(f32[128,10,256]{2,1,0:T(8,128)S(1)} %bitcast.127), channel_id=1, replica_groups=mesh['mem'=8,'grid'=16] {'mem','grid'}, dimensions={0} | all-to-all | bytes 2621440 | tf_op jit(solution)/shard_map/all_to_all | solution.py:62
  683.6 0.8 copy.79
  684.3 0.2 pad.4
  684.5 2.5 copy.97
  (93 shorter events, 2.0 us)
Async XLA Ops:
  11.0 11.6 %copy-start.8 = (s32[4]{0:T(128)S(1)}, s32[4]{0:T(128)}, u32[]{:S(2)}) copy-start(s32[4]{0:T(128)} %param.15) | copy-start | bytes 52
  11.0 19.8 %copy-start.7 = (s32[4]{0:T(128)S(1)}, s32[4]{0:T(128)}, u32[]{:S(2)}) copy-start(s32[4]{0:T(128)} %param.10) | copy-start | bytes 52
  11.0 23.2 %copy-start.9 = (s32[4,256]{1,0:T(4,128)S(1)}, s32[4,256]{1,0:T(4,128)}, u32[]{:S(2)}) copy-start(s32[4,256]{1,0:T(4,128)} %param.11) | copy-start | bytes 12292
  11.0 23.2 %copy-start.6 = (s32[4,4096]{1,0:T(4,128)S(1)}, s32[4,4096]{1,0:T(4,128)}, u32[]{:S(2)}) copy-start(s32[4,4096]{1,0:T(4,128)} %param.14) | copy-start | bytes 196612
  11.0 41.3 %all-to-all-start = ((f32[10,128,256]{2,0,1:T(8,128)}), f32[10,128,256]{2,0,1:T(8,128)S(1)}, u32[]{:S(2)}, u32[]{:S(2)}) async-start(f32[10,128,256]{2,0,1:T(8,128)} %copy.62), calls=%async_computation | async-start | bytes 4194304 | tf_op jit(solution)/shard_map/all_to_all | solution.py:26
  22.5 166.1 %all-reduce.5.cloned.1.call-start = ((), (), s32[]{:S(2)}) async-start(), calls=%async_computation.2 | async-start | bytes 163840 | tf_op jit(solution)/shard_map/psum | solution.py:12
  53.9 285.5 %all-reduce.7.cloned.1.call-start = ((), (), s32[]{:S(2)}) async-start(), calls=%async_computation.3 | async-start | bytes 163840 | tf_op jit(solution)/shard_map/psum | solution.py:12
  54.9 135.6 %copy-start.10 = (f32[4,256]{1,0:T(4,128)S(1)}, f32[4,256]{1,0:T(4,128)}, u32[]{:S(2)}) copy-start(f32[4,256]{1,0:T(4,128)} %param.12) | copy-start | bytes 12292
  54.9 135.5 %copy-start.11 = (f32[4,256]{1,0:T(4,128)S(1)}, f32[4,256]{1,0:T(4,128)}, u32[]{:S(2)}) copy-start(f32[4,256]{1,0:T(4,128)} %param.13) | copy-start | bytes 12292
  201.0 1.3 copy-start
  202.4 139.8 %copy-start.1 = (f32[8,16,10,256]{3,2,1,0:T(8,128)S(1)}, f32[8,16,10,256]{3,2,1,0:T(8,128)}, u32[]{:S(2)}) copy-start(f32[8,16,10,256]{3,2,1,0:T(8,128)} %copy-done) | copy-start | bytes 3932164
  204.0 284.6 %all-reduce.9.cloned.1.call-start = ((), (), s32[]{:S(2)}) async-start(), calls=%async_computation.4 | async-start | bytes 163840 | tf_op jit(solution)/shard_map/psum | solution.py:12
  350.2 1.3 copy-start.2
  351.6 139.8 %copy-start.3 = (f32[8,16,10,256]{3,2,1,0:T(8,128)S(1)}, f32[8,16,10,256]{3,2,1,0:T(8,128)}, u32[]{:S(2)}) copy-start(f32[8,16,10,256]{3,2,1,0:T(8,128)} %copy-done.2) | copy-start | bytes 3932164
  353.2 284.6 %all-reduce.11.cloned.1.call-start = ((), (), s32[]{:S(2)}) async-start(), calls=%async_computation.5 | async-start | bytes 163840 | tf_op jit(solution)/shard_map/psum | solution.py:12
  499.4 1.3 copy-start.4
  500.8 139.8 %copy-start.5 = (f32[8,16,10,256]{3,2,1,0:T(8,128)S(1)}, f32[8,16,10,256]{3,2,1,0:T(8,128)}, u32[]{:S(2)}) copy-start(f32[8,16,10,256]{3,2,1,0:T(8,128)} %copy-done.4) | copy-start | bytes 3932164
Sparse Core Ops, SparseCore 0:
  54.0 134.5 all-reduce.4
  204.1 135.2 all-reduce.6
  353.3 135.1 all-reduce.8
  502.5 135.2 all-reduce.10
where the time goes:
time: 699 us; the launch traced here: 694 us
  waiting for transfers between devices  550 us (79%)
  blocking collectives  34.7 us (5%)
  matrix products  33.6 us (5%)
  between operations  24.4 us (3%)
  local copies, waits for them, and re-layouts  22.6 us (3%)
  other arithmetic  15.8 us (2%)
  starting transfers between devices  12.6 us (2%)
    psum x4, waiting for transfers between devices, from_root(): return lax.psum(jnp.where(mine, value, jnp.zeros_like(value)), axis)  538 us
    all_to_all x1, blocking collectives, on_device(): lax.all_to_all(flat, ('mem', 'grid'), split_axis=0, concat_axis=1, tiled=...  34.7 us
    dot_general x4, matrix products, on_device(): incr = jnp.einsum('gpo,amo->agmp', coef, dy_inc, precision=highest)  17.9 us
    dot_general x4, matrix products, on_device(): coef = jnp.einsum('agmp,amo->gpo', anom, weighted, precision=highest)  15.7 us
  transfers between devices with their start and end apart: 5, of which 5 were waited for; matrix products, arithmetic and copies ran while one was open for 1% of the time, Pallas kernels for 0%

commit v1 on v0

v1 whole, which is shorter than its diff:
```python
import jax
import jax.numpy as jnp
from jax import lax
from jax.experimental import pallas as pl
from jax.experimental.pallas import tpu as pltpu
from jax.sharding import PartitionSpec as P

MESH = pl.DeviceIdType.MESH
F32, BF16 = jnp.float32, jnp.bfloat16

MEM = 8
GX, GY = 4, 4
ROWS = 10
M = MEM * ROWS
OBS = 256
BLOCKS = 4
TILE = 128
QUAD = 4
CHUNKS = 4
QUADS = 2
WIDTH = QUADS * QUAD * TILE
OWN = CHUNKS * WIDTH
LOCAL = MEM * OWN
KDIM = 256


def split(x):
    hi = x.astype(BF16)
    lo = (x - hi.astype(F32)).astype(BF16)
    return hi, lo


def stacked(x):
    hi, lo = split(x)
    return jnp.concatenate([hi, lo, hi, jnp.zeros((KDIM - 3 * M, x.shape[1]), BF16)], axis=0)


def left_form(tri):
    hi, lo = split(tri)
    lane = lax.broadcasted_iota(jnp.int32, tri.shape, 1)
    return jnp.where(lane < 2 * M, hi.astype(F32), lo.astype(F32)).astype(BF16)


def dot(a, b):
    return jnp.dot(a, b, preferred_element_type=F32)


def dot_nt(a, b):
    return lax.dot_general(a, b, (((1,), (1,)), ((), ())), preferred_element_type=F32)


def pairs_transposed(regs):
    pair = lax.broadcasted_iota(jnp.int32, (8, TILE), 0) // 2
    out = []
    for j in range(QUAD):
        acc = None
        for i in range(QUAD):
            moved = regs[i] if i == j else pltpu.roll(regs[i], (2 * (i - j)) % 8, 0)
            acc = moved if acc is None else jnp.where(pair == i, moved, acc)
        out.append(acc)
    return out


def gathered_quad(load):
    tails = [pairs_transposed([load(4 * h + s, QUAD) for s in range(4)]) for h in range(2)]
    tiles = []
    for t in range(QUAD):
        tiles.append(jnp.concatenate([load(s, t) for s in range(MEM)] + [tails[0][t], tails[1][t]], axis=0))
    return tiles


def kernel(
    x_hbm, tile_ref, order_ref, off_ref, val_ref, err_ref, mask_ref,
    out_hbm,
    x_v, o_v, send1, recv1, send2, recv2, slab_a, slab_b, slab_c, got_x, got_y, got_m, hc, amat,
    x_sem, o_sem, ssem1, rsem1, ssem2, rsem2, xs, xr, ys, yr, ms, mr,
):
    me = lax.axis_index("mem")
    g = lax.axis_index("grid")
    gx, gy = g // GY, lax.rem(g, GY)

    load_x = pltpu.make_async_copy(x_hbm, x_v, x_sem)
    load_x.start()

    def remote(src, dst, s, r, peer):
        return pltpu.make_async_remote_copy(
            src_ref=src, dst_ref=dst, send_sem=s, recv_sem=r, device_id=peer, device_id_type=MESH
        )

    mem_peers = [{"mem": lax.rem(me + k, MEM)} for k in range(1, MEM)]
    x_peers = [{"grid": lax.rem(gx + k, GX) * GY + gy} for k in range(1, GX)]
    y_peers = [{"grid": gx * GY + lax.rem(gy + k, GY)} for k in range(1, GY)]
    barrier = pltpu.get_barrier_semaphore()
    for peer in mem_peers + x_peers + y_peers:
        pl.semaphore_signal(barrier, inc=1, device_id=peer, device_id_type=MESH)

    load_x.wait()

    blocks = [order_ref[k] for k in range(BLOCKS)]
    tiles = [tile_ref[blocks[k]] for k in range(BLOCKS)]
    per = LOCAL // TILE
    for k in range(BLOCKS):
        within = lax.rem(tiles[k], per)
        start = within * TILE
        away = tiles[k] - within - g * per
        mine = jnp.full((8, TILE), away, jnp.int32) == 0
        slab_a[k] = jnp.where(mine, x_v[0:8, pl.ds(start, TILE)], 0.0)
        slab_a[QUAD, 2 * k : 2 * k + 2, :] = jnp.where(mine[0:2], x_v[8:10, pl.ds(start, TILE)], 0.0)

    def pack(q):
        def step(d, c):
            for u in range(QUADS):
                for t in range(QUAD):
                    col = pl.multiple_of(d * OWN + q * WIDTH + (u * QUAD + t) * TILE, TILE)
                    send1[d, q, u, t] = x_v[0:8, pl.ds(col, TILE)]
                    send1[d, q, u, QUAD, 2 * t : 2 * t + 2, :] = x_v[8:10, pl.ds(col, TILE)]
            return c

        lax.fori_loop(0, MEM, step, 0)

    def out1(q, k):
        peer = mem_peers[k]
        return remote(send1.at[peer["mem"], q], recv1.at[me, q], ssem1.at[q, k], rsem1.at[q, k], peer)

    def push(q):
        for k in range(MEM - 1):
            out1(q, k).start()

    pack(0)
    pl.semaphore_wait(barrier, MEM - 1 + GX - 1 + GY - 1)

    cx = [remote(slab_a, got_x.at[k], xs.at[k], xr.at[k], x_peers[k]) for k in range(GX - 1)]
    for c in cx:
        c.start()
    push(0)
    pack(1)
    push(1)
    for c in cx:
        c.wait()
    slab_b[...] = slab_a[...] + got_x[0] + got_x[1] + got_x[2]
    cy = [remote(slab_b, got_y.at[k], ys.at[k], yr.at[k], y_peers[k]) for k in range(GY - 1)]
    for c in cy:
        c.start()
    pack(2)
    push(2)
    for c in cy:
        c.wait()
    slab_c[...] = slab_b[...] + got_y[0] + got_y[1] + got_y[2]
    cm = [remote(slab_c, got_m.at[me], ms.at[k], mr.at[k], mem_peers[k]) for k in range(MEM - 1)]
    for c in cm:
        c.start()
    got_m[me] = slab_c[...]
    pack(3)
    push(3)
    for c in cm:
        c.wait()

    slabs = gathered_quad(lambda s, t: got_m[s, t])
    lane = lax.broadcasted_iota(jnp.int32, (M, KDIM), 1)
    row = lax.broadcasted_iota(jnp.int32, (M, KDIM), 0)
    eye = jnp.where(lax.rem(lane, M) == row, 1.0, 0.0).astype(F32)
    amat[0] = eye
    hc[0] = jnp.zeros((M, KDIM), BF16)
    for k in range(BLOCKS):
        b = blocks[k]
        off = off_ref[pl.ds(b, 1), :]
        val = val_ref[pl.ds(b, 1), :]
        err = err_ref[pl.ds(b, 1), :]
        sublane = lax.broadcasted_iota(jnp.int32, (TILE, OBS), 0)
        hot = jnp.where(sublane == off, 1.0, 0.0).astype(BF16)
        top, rest = split(slabs[k])
        low = (slabs[k] - top.astype(F32) - rest.astype(F32)).astype(BF16)
        prior = dot(top, hot) + (dot(rest, hot) + dot(low, hot))
        ybar = jnp.sum(prior, axis=0, keepdims=True) * (1.0 / M)
        dev = prior - ybar
        var = jnp.sum(dev * dev, axis=0, keepdims=True) * (1.0 / (M - 1.0))
        total = var + err
        lead = var / total * (val - ybar)
        shrink = jnp.sqrt(err / total) - 1.0
        dy = lead + shrink * dev
        weighted = dev * (1.0 / ((M - 1.0) * (var + 1e-05)))
        dh, dl = split(dy)
        wh, wl = split(weighted)
        pad = jnp.zeros((KDIM - 3 * M, OBS), BF16)
        wh = jnp.concatenate([wh, wh, wh, pad], axis=0)
        wl = jnp.concatenate([wl, wl, wl, pad], axis=0)
        tri = dot_nt(dh, wh) + (dot_nt(dh, wl) + dot_nt(dl, wh))
        left = left_form(tri)
        for j in range(k + 1, BLOCKS):
            on = mask_ref[b, tiles[j]].astype(F32)
            slabs[j] = slabs[j] + on * dot(left, stacked(slabs[j]))
        for p in range(1 << k):
            base = amat[p]
            new = base + (tri if p == 0 else dot(left, stacked(base)))
            if k < BLOCKS - 1:
                amat[(1 << k) + p] = new
            hc[(1 << k) + p] = left_form(new - eye)

    def out2(q, k):
        peer = mem_peers[k]
        return remote(send2.at[peer["mem"], q], recv2.at[me, q], ssem2.at[q, k], rsem2.at[q, k], peer)

    first_tile = g * per + me * (OWN // TILE)

    def own_copy(q, c):
        recv1[me, q] = send1[me, q]
        return c

    lax.fori_loop(0, CHUNKS, own_copy, 0)

    def update(q, c):
        for k in range(MEM - 1):
            out1(q, k).wait()
        for u in range(QUADS):
            xs_ = gathered_quad(lambda s, t: recv1[s, q, u, t])
            tails = [[], []]
            for t in range(QUAD):
                tile = first_tile + q * (QUADS * QUAD) + (u * QUAD + t)
                pattern = jnp.int32(0)
                for k in range(BLOCKS):
                    pattern = pattern + mask_ref[blocks[k], tile] * (1 << k)
                y = xs_[t] + dot(hc[pattern], stacked(xs_[t]))
                for d in range(MEM):
                    send2[d, q, u, t] = y[8 * d : 8 * d + 8]
                for h in range(2):
                    tails[h].append(y[8 * MEM + 8 * h : 8 * MEM + 8 * h + 8])
            for h in range(2):
                back = pairs_transposed(tails[h])
                for d in range(4):
                    send2[4 * h + d, q, u, QUAD] = back[d]
        for k in range(MEM - 1):
            out2(q, k).start()
        recv2[me, q] = send2[me, q]
        return c

    lax.fori_loop(0, CHUNKS, update, 0)

    def finish(q, c):
        for k in range(MEM - 1):
            out2(q, k).wait()

        def step(d, c):
            for u in range(QUADS):
                for t in range(QUAD):
                    col = pl.multiple_of(d * OWN + q * WIDTH + (u * QUAD + t) * TILE, TILE)
                    o_v[0:8, pl.ds(col, TILE)] = recv2[d, q, u, t]
                    o_v[8:10, pl.ds(col, TILE)] = recv2[d, q, u, QUAD, 2 * t : 2 * t + 2, :]
            return c

        lax.fori_loop(0, MEM, step, 0)
        return c

    lax.fori_loop(0, CHUNKS, finish, 0)
    store = pltpu.make_async_copy(o_v, out_hbm, o_sem)
    store.start()
    store.wait()


def on_device(state, obs_tile, obs_offset, obs_value, obs_error, loc_mask, block_order):
    piece = (QUADS, QUAD + 1, 8, TILE)
    whole = (MEM, CHUNKS) + piece
    slab = (QUAD + 1, 8, TILE)
    smem = pl.BlockSpec(memory_space=pltpu.SMEM)
    vmem = pl.BlockSpec(memory_space=pltpu.VMEM)
    anyw = pl.BlockSpec(memory_space=pl.ANY)
    dma = pltpu.SemaphoreType.DMA
    return pl.pallas_call(
        kernel,
        out_shape=jax.ShapeDtypeStruct(state.shape, F32),
        in_specs=[anyw, smem, smem, vmem, vmem, vmem, smem],
        out_specs=anyw,
        scratch_shapes=[
            pltpu.VMEM((ROWS, LOCAL), F32),
            pltpu.VMEM((ROWS, LOCAL), F32),
            pltpu.VMEM(whole, F32),
            pltpu.VMEM(whole, F32),
            pltpu.VMEM(whole, F32),
            pltpu.VMEM(whole, F32),
            pltpu.VMEM(slab, F32),
            pltpu.VMEM(slab, F32),
            pltpu.VMEM(slab, F32),
            pltpu.VMEM((GX - 1,) + slab, F32),
            pltpu.VMEM((GY - 1,) + slab, F32),
            pltpu.VMEM((MEM,) + slab, F32),
            pltpu.VMEM((1 << BLOCKS, M, KDIM), BF16),
            pltpu.VMEM((1 << (BLOCKS - 1), M, KDIM), F32),
            dma, dma,
            dma((CHUNKS, MEM - 1)), dma((CHUNKS, MEM - 1)),
            dma((CHUNKS, MEM - 1)), dma((CHUNKS, MEM - 1)),
            dma((GX - 1,)), dma((GX - 1,)),
            dma((GY - 1,)), dma((GY - 1,)),
            dma((MEM - 1,)), dma((MEM - 1,)),
        ],
        compiler_params=pltpu.CompilerParams(
            collective_id=0, has_side_effects=True, vmem_limit_bytes=40 << 20
        ),
        name="ensemble_update",
    )(state, obs_tile, block_order, obs_offset, obs_value, obs_error, loc_mask)


def solution(mesh):
    placed = (P("mem", "grid"), P(), P(), P(), P(), P(), P())
    return jax.shard_map(
        on_device, mesh=mesh, in_specs=placed, out_specs=P("mem", "grid"), check_vma=False
    )
```

time: 699 us -> 52.5 us (0.08)
  waiting for transfers between devices: 550 us -> 0 us
  Pallas kernels: 0 us -> 45.1 us
  blocking collectives: 34.7 us -> 0 us
  matrix products: 33.6 us -> 0 us
  between operations: 24.4 us -> 0.02 us
  other arithmetic: 15.8 us -> 0 us
  local copies, waits for them, and re-layouts: 22.6 us -> 7.12 us
  starting transfers between devices: 12.6 us -> 0 us
    psum x4 -> x0, waiting for transfers between devices: 538 us -> none  [from_root(): return lax.psum(jnp.where(mine, value, jnp.zeros_like(value)), axis)]
    pallas_call x0 -> x1, Pallas kernels: none -> 45.1 us  [on_device(): pl.pallas_call(kernel, out_shape=jax.ShapeDtypeStruct(state.shape, F32),...]
    all_to_all x1 -> x0, blocking collectives: 34.7 us -> none  [on_device(): lax.all_to_all(flat, ('mem', 'grid'), split_axis=0, concat_axis=1, tiled=...]
    dot_general x8 -> x0, matrix products: 33.6 us -> none  [the longest x4 17.9 us: on_device(): incr = jnp.einsum('gpo,amo->agmp', coef, dy_inc, precision=highest)]
    all_to_all x1 -> x0, waiting for transfers between devices: 12.4 us -> none  [on_device(): lax.all_to_all(state, ('mem', 'grid'), split_axis=1, concat_axis=0, tiled...]
    all_to_all x1 -> x0, starting transfers between devices: 11.5 us -> none  [on_device(): lax.all_to_all(state, ('mem', 'grid'), split_axis=1, concat_axis=0, tiled...]
    reduce_sum x10 -> x0, other arithmetic: 7.68 us -> none  [the longest x4 3.66 us: on_device(): var = jnp.sum(dev * dev, axis=0) / (members - 1.0)]
  transfers between devices with their start and end apart: 5 -> 0, of which waited for: 5 -> 0; matrix products, arithmetic and copies ran while one was open for 1% -> 0% of each run, Pallas kernels for 0% -> 0%
where the time goes in v1:
time: 52.5 us; the launch traced here: 52.2 us
  Pallas kernels  45.1 us (86%)
  local copies, waits for them, and re-layouts  7.12 us (14%)
    pallas_call x1, Pallas kernels, on_device(): pl.pallas_call(kernel, out_shape=jax.ShapeDtypeStruct(state.shape, F32),...  45.1 us
    unnamed x15, local copies, waits for them, and re-layouts  7.12 us

profile of v1, /device:TPU:1, one launch (start us, length us, event | category | flops | bytes accessed | tf_op | source)
XLA Modules:
  0.0 52.2 jit_solution(1507581235400312444)
XLA Ops:
  0.0 0.0 copy-start
  0.0 1.6 %copy-done = f32[10,32768]{1,0:T(8,128)S(1)} copy-done((f32[10,32768]{1,0:T(8,128)S(1)}, f32[10,32768]{1,0:T(8,128)}, u32[]{:S(2)}) %copy-start) | copy-done | bytes 1310744
  1.6 0.0 copy-start.1
  1.6 0.8 %copy-done.1 = s32[4,4096]{1,0:T(4,128)S(1)} copy-done((s32[4,4096]{1,0:T(4,128)S(1)}, s32[4,4096]{1,0:T(4,128)}, u32[]{:S(2)}) %copy-start.1) | copy-done | bytes 65560
  2.4 0.0 copy-start.2
  2.4 0.7 %copy-done.2 = s32[4,256]{1,0:T(4,128)S(1)} copy-done((s32[4,256]{1,0:T(4,128)S(1)}, s32[4,256]{1,0:T(4,128)}, u32[]{:S(2)}) %copy-start.2) | copy-done | bytes 4120
  3.1 0.0 copy-start.3
  3.1 0.7 %copy-done.3 = f32[4,256]{1,0:T(4,128)S(1)} copy-done((f32[4,256]{1,0:T(4,128)S(1)}, f32[4,256]{1,0:T(4,128)}, u32[]{:S(2)}) %copy-start.3) | copy-done | bytes 4120
  3.8 0.0 copy-start.4
  3.8 0.7 %copy-done.4 = f32[4,256]{1,0:T(4,128)S(1)} copy-done((f32[4,256]{1,0:T(4,128)S(1)}, f32[4,256]{1,0:T(4,128)}, u32[]{:S(2)}) %copy-start.4) | copy-done | bytes 4120
  4.5 0.0 copy-start.5
  4.5 0.7 %copy-done.5 = s32[4]{0:T(128)S(1)} copy-done((s32[4]{0:T(128)S(1)}, s32[4]{0:T(128)}, u32[]{:S(2)}) %copy-start.5) | copy-done | bytes 40
  5.2 0.0 copy-start.6
  5.2 0.7 %copy-done.6 = s32[4]{0:T(128)S(1)} copy-done((s32[4]{0:T(128)S(1)}, s32[4]{0:T(128)}, u32[]{:S(2)}) %copy-start.6) | copy-done | bytes 40
  5.8 45.1 %ensemble_update.1 = f32[10,32768]{1,0:T(8,128)S(1)} custom-call(f32[10,32768]{1,0:T(8,128)S(1)} %copy-done, s32[4]{0:T(128)S(1)} %copy-done.5, s32[4]{0:T(128)S(1)} %copy-done.6, s32[4,256]{1,0:T(4,128)S(1)} %copy-done.2, f32[4,256]{1,0:T(4,128)S(1)} %copy-done.3, f32[4,256]{1,0:T(4,128)S(1)} %copy-done.4, s32[4,4096]{1,0:T(4,128)S(1)} %copy-done.1), custom_call_target="tpu_custom_call" | custom-call | tf_op jit(solution)/shard_map/ensemble_update/pallas_call | solution.py:267
  50.9 1.3 %copy.9 = f32[10,32768]{1,0:T(8,128)} copy(f32[10,32768]{1,0:T(8,128)S(1)} %ensemble_update.1) | data formatting | bytes 2621440
Async XLA Ops:
  0.0 1.6 %copy-start = (f32[10,32768]{1,0:T(8,128)S(1)}, f32[10,32768]{1,0:T(8,128)}, u32[]{:S(2)}) copy-start(f32[10,32768]{1,0:T(8,128)} %x_hbm.1) | copy-start | bytes 3932164
  1.6 0.8 %copy-start.1 = (s32[4,4096]{1,0:T(4,128)S(1)}, s32[4,4096]{1,0:T(4,128)}, u32[]{:S(2)}) copy-start(s32[4,4096]{1,0:T(4,128)} %mask_ref.1) | copy-start | bytes 196612
  2.4 0.7 %copy-start.2 = (s32[4,256]{1,0:T(4,128)S(1)}, s32[4,256]{1,0:T(4,128)}, u32[]{:S(2)}) copy-start(s32[4,256]{1,0:T(4,128)} %off_ref.1) | copy-start | bytes 12292
  3.1 0.7 %copy-start.3 = (f32[4,256]{1,0:T(4,128)S(1)}, f32[4,256]{1,0:T(4,128)}, u32[]{:S(2)}) copy-start(f32[4,256]{1,0:T(4,128)} %val_ref.1) | copy-start | bytes 12292
  3.8 0.7 %copy-start.4 = (f32[4,256]{1,0:T(4,128)S(1)}, f32[4,256]{1,0:T(4,128)}, u32[]{:S(2)}) copy-start(f32[4,256]{1,0:T(4,128)} %err_ref.1) | copy-start | bytes 12292
  4.5 0.7 %copy-start.5 = (s32[4]{0:T(128)S(1)}, s32[4]{0:T(128)}, u32[]{:S(2)}) copy-start(s32[4]{0:T(128)} %tile_ref.1) | copy-start | bytes 52
  5.2 0.7 %copy-start.6 = (s32[4]{0:T(128)S(1)}, s32[4]{0:T(128)}, u32[]{:S(2)}) copy-start(s32[4]{0:T(128)} %order_ref.1) | copy-start | bytes 52

commit v2 on v1

--- a/solution.py
+++ b/solution.py
@@ -21,6 +21,7 @@
 WIDTH = QUADS * QUAD * TILE
 OWN = CHUNKS * WIDTH
 LOCAL = MEM * OWN
+PACKED = WIDTH + QUADS * TILE
 KDIM = 256
 
 
@@ -61,26 +62,28 @@
     return out
 
 
-def gathered_quad(load):
-    tails = [pairs_transposed([load(4 * h + s, QUAD) for s in range(4)]) for h in range(2)]
+def gathered_quad(main, tail):
+    tails = [pairs_transposed([tail(4 * h + s) for s in range(4)]) for h in range(2)]
     tiles = []
     for t in range(QUAD):
-        tiles.append(jnp.concatenate([load(s, t) for s in range(MEM)] + [tails[0][t], tails[1][t]], axis=0))
+        tiles.append(jnp.concatenate([main(s, t) for s in range(MEM)] + [tails[0][t], tails[1][t]], axis=0))
     return tiles
 
 
+def lanes(tile):
+    return pl.ds(tile * TILE, TILE)
+
+
 def kernel(
-    x_hbm, tile_ref, order_ref, off_ref, val_ref, err_ref, mask_ref,
-    out_hbm,
-    x_v, o_v, send1, recv1, send2, recv2, slab_a, slab_b, slab_c, got_x, got_y, got_m, hc, amat,
-    x_sem, o_sem, ssem1, rsem1, ssem2, rsem2, xs, xr, ys, yr, ms, mr,
+    x_hbm, tile_hbm, order_hbm, off_hbm, val_hbm, err_hbm, mask_hbm,
+    recv2,
+    x_v, tile_ref, order_ref, off_ref, val_ref, err_ref, mask_ref,
+    tails, recv1, send2, slab_a, slab_b, slab_c, got_x, got_y, got_m, hc, amat,
+    x_sem, in_sem, own_sem, ssem1, rsem1, tsend, trecv, ssem2, rsem2, xs, xr, ys, yr, ms, mr,
 ):
     me = lax.axis_index("mem")
     g = lax.axis_index("grid")
     gx, gy = g // GY, lax.rem(g, GY)
-
-    load_x = pltpu.make_async_copy(x_hbm, x_v, x_sem)
-    load_x.start()
 
     def remote(src, dst, s, r, peer):
         return pltpu.make_async_remote_copy(
@@ -94,6 +97,37 @@
     for peer in mem_peers + x_peers + y_peers:
         pl.semaphore_signal(barrier, inc=1, device_id=peer, device_id_type=MESH)
 
+    small = [
+        pltpu.make_async_copy(src, dst, in_sem.at[i])
+        for i, (src, dst) in enumerate([
+            (order_hbm, order_ref), (tile_hbm, tile_ref), (mask_hbm, mask_ref),
+            (off_hbm, off_ref), (val_hbm, val_ref), (err_hbm, err_ref),
+        ])
+    ]
+    load_x = pltpu.make_async_copy(x_hbm, x_v, x_sem)
+    load_x.start()
+    for c in small:
+        c.start()
+
+    def columns(d, q):
+        return pl.ds(pl.multiple_of(d * OWN + q * WIDTH, WIDTH), WIDTH)
+
+    def out1(q, k):
+        peer = mem_peers[k]
+        src = x_hbm.at[0:8, columns(peer["mem"], q)]
+        return remote(src, recv1.at[me, q, :, 0:WIDTH], ssem1.at[q, k], rsem1.at[q, k], peer)
+
+    def out_tails(k):
+        peer = mem_peers[k]
+        dst = recv1.at[me, :, :, WIDTH:PACKED]
+        return remote(tails.at[peer["mem"]], dst, tsend.at[k], trecv.at[k], peer)
+
+    def push(q):
+        for k in range(MEM - 1):
+            out1(q, k).start()
+
+    for c in small:
+        c.wait()
     load_x.wait()
 
     blocks = [order_ref[k] for k in range(BLOCKS)]
@@ -107,42 +141,30 @@
         slab_a[k] = jnp.where(mine, x_v[0:8, pl.ds(start, TILE)], 0.0)
         slab_a[QUAD, 2 * k : 2 * k + 2, :] = jnp.where(mine[0:2], x_v[8:10, pl.ds(start, TILE)], 0.0)
 
-    def pack(q):
-        def step(d, c):
+    pl.semaphore_wait(barrier, MEM - 1 + GX - 1 + GY - 1)
+
+    cx = [remote(slab_a, got_x.at[k], xs.at[k], xr.at[k], x_peers[k]) for k in range(GX - 1)]
+    for c in cx:
+        c.start()
+    push(0)
+
+    def pack(d, c):
+        for q in range(CHUNKS):
             for u in range(QUADS):
                 for t in range(QUAD):
                     col = pl.multiple_of(d * OWN + q * WIDTH + (u * QUAD + t) * TILE, TILE)
-                    send1[d, q, u, t] = x_v[0:8, pl.ds(col, TILE)]
-                    send1[d, q, u, QUAD, 2 * t : 2 * t + 2, :] = x_v[8:10, pl.ds(col, TILE)]
-            return c
-
-        lax.fori_loop(0, MEM, step, 0)
-
-    def out1(q, k):
-        peer = mem_peers[k]
-        return remote(send1.at[peer["mem"], q], recv1.at[me, q], ssem1.at[q, k], rsem1.at[q, k], peer)
-
-    def push(q):
-        for k in range(MEM - 1):
-            out1(q, k).start()
-
-    pack(0)
-    pl.semaphore_wait(barrier, MEM - 1 + GX - 1 + GY - 1)
-
-    cx = [remote(slab_a, got_x.at[k], xs.at[k], xr.at[k], x_peers[k]) for k in range(GX - 1)]
-    for c in cx:
-        c.start()
-    push(0)
-    pack(1)
-    push(1)
+                    tails[d, q, 2 * t : 2 * t + 2, u * TILE : (u + 1) * TILE] = x_v[8:10, pl.ds(col, TILE)]
+        return c
+
+    lax.fori_loop(0, MEM, pack, 0)
     for c in cx:
         c.wait()
     slab_b[...] = slab_a[...] + got_x[0] + got_x[1] + got_x[2]
     cy = [remote(slab_b, got_y.at[k], ys.at[k], yr.at[k], y_peers[k]) for k in range(GY - 1)]
     for c in cy:
         c.start()
-    pack(2)
-    push(2)
+    for k in range(MEM - 1):
+        out_tails(k).start()
     for c in cy:
         c.wait()
     slab_c[...] = slab_b[...] + got_y[0] + got_y[1] + got_y[2]
@@ -150,12 +172,19 @@
     for c in cm:
         c.start()
     got_m[me] = slab_c[...]
-    pack(3)
-    push(3)
+    for q in range(1, CHUNKS):
+        push(q)
+    own = [
+        pltpu.make_async_copy(x_hbm.at[0:8, columns(me, q)], recv1.at[me, q, :, 0:WIDTH], own_sem.at[q])
+        for q in range(CHUNKS)
+    ]
+    for c in own:
+        c.start()
+    recv1[me, :, :, WIDTH:PACKED] = tails[me]
     for c in cm:
         c.wait()
 
-    slabs = gathered_quad(lambda s, t: got_m[s, t])
+    slabs = gathered_quad(lambda s, t: got_m[s, t], lambda s: got_m[s, QUAD])
     lane = lax.broadcasted_iota(jnp.int32, (M, KDIM), 1)
     row = lax.broadcasted_iota(jnp.int32, (M, KDIM), 0)
     eye = jnp.where(lax.rem(lane, M) == row, 1.0, 0.0).astype(F32)
@@ -196,84 +225,96 @@
                 amat[(1 << k) + p] = new
             hc[(1 << k) + p] = left_form(new - eye)
 
+    for c in own:
+        c.wait()
+    for k in range(MEM - 1):
+        out_tails(k).wait()
+
     def out2(q, k):
         peer = mem_peers[k]
         return remote(send2.at[peer["mem"], q], recv2.at[me, q], ssem2.at[q, k], rsem2.at[q, k], peer)
 
+    def keep(q):
+        return pltpu.make_async_copy(send2.at[me, q], recv2.at[me, q], own_sem.at[q])
+
     first_tile = g * per + me * (OWN // TILE)
-
-    def own_copy(q, c):
-        recv1[me, q] = send1[me, q]
-        return c
-
-    lax.fori_loop(0, CHUNKS, own_copy, 0)
 
     def update(q, c):
         for k in range(MEM - 1):
             out1(q, k).wait()
         for u in range(QUADS):
-            xs_ = gathered_quad(lambda s, t: recv1[s, q, u, t])
-            tails = [[], []]
+            quad = gathered_quad(
+                lambda s, t: recv1[s, q, :, lanes(u * QUAD + t)], lambda s: recv1[s, q, :, lanes(QUADS * QUAD + u)]
+            )
+            pairs = [[], []]
             for t in range(QUAD):
                 tile = first_tile + q * (QUADS * QUAD) + (u * QUAD + t)
                 pattern = jnp.int32(0)
                 for k in range(BLOCKS):
                     pattern = pattern + mask_ref[blocks[k], tile] * (1 << k)
-                y = xs_[t] + dot(hc[pattern], stacked(xs_[t]))
+                y = quad[t] + dot(hc[pattern], stacked(quad[t]))
                 for d in range(MEM):
-                    send2[d, q, u, t] = y[8 * d : 8 * d + 8]
+                    send2[d, q, :, lanes(u * QUAD + t)] = y[8 * d : 8 * d + 8]
                 for h in range(2):
-                    tails[h].append(y[8 * MEM + 8 * h : 8 * MEM + 8 * h + 8])
+                    pairs[h].append(y[8 * MEM + 8 * h : 8 * MEM + 8 * h + 8])
             for h in range(2):
-                back = pairs_transposed(tails[h])
+                back = pairs_transposed(pairs[h])
                 for d in range(4):
-                    send2[4 * h + d, q, u, QUAD] = back[d]
+                    send2[4 * h + d, q, :, lanes(QUADS * QUAD + u)] = back[d]
         for k in range(MEM - 1):
             out2(q, k).start()
-        recv2[me, q] = send2[me, q]
+        keep(q).start()
         return c
 
     lax.fori_loop(0, CHUNKS, update, 0)
-
-    def finish(q, c):
+    for q in range(CHUNKS):
+        keep(q).wait()
         for k in range(MEM - 1):
             out2(q, k).wait()
 
-        def step(d, c):
+
+def unpack(packed, out, held, rows_v, in_sem, main_sem, row_sem):
+    loads = [pltpu.make_async_copy(packed.at[d], held.at[d], in_sem.at[d]) for d in range(MEM)]
+    for c in loads:
+        c.start()
+    started = []
+    for d in range(MEM):
+        loads[d].wait()
+        for q in range(CHUNKS):
+            cols = pl.ds(d * OWN + q * WIDTH, WIDTH)
+            started.append(pltpu.make_async_copy(held.at[d, q, :, 0:WIDTH], out.at[0:8, cols], main_sem.at[d, q]))
+            started[-1].start()
+        for q in range(CHUNKS):
             for u in range(QUADS):
                 for t in range(QUAD):
-                    col = pl.multiple_of(d * OWN + q * WIDTH + (u * QUAD + t) * TILE, TILE)
-                    o_v[0:8, pl.ds(col, TILE)] = recv2[d, q, u, t]
-                    o_v[8:10, pl.ds(col, TILE)] = recv2[d, q, u, QUAD, 2 * t : 2 * t + 2, :]
-            return c
-
-        lax.fori_loop(0, MEM, step, 0)
-        return c
-
-    lax.fori_loop(0, CHUNKS, finish, 0)
-    store = pltpu.make_async_copy(o_v, out_hbm, o_sem)
-    store.start()
-    store.wait()
+                    col = d * OWN + q * WIDTH + (u * QUAD + t) * TILE
+                    rows_v[:, col : col + TILE] = held[d, q, 2 * t : 2 * t + 2, WIDTH + u * TILE : WIDTH + (u + 1) * TILE]
+        cols = pl.ds(d * OWN, OWN)
+        started.append(pltpu.make_async_copy(rows_v.at[:, cols], out.at[8:10, cols], row_sem.at[d]))
+        started[-1].start()
+    for c in started:
+        c.wait()
 
 
 def on_device(state, obs_tile, obs_offset, obs_value, obs_error, loc_mask, block_order):
-    piece = (QUADS, QUAD + 1, 8, TILE)
-    whole = (MEM, CHUNKS) + piece
+    whole = (MEM, CHUNKS, 8, PACKED)
     slab = (QUAD + 1, 8, TILE)
-    smem = pl.BlockSpec(memory_space=pltpu.SMEM)
-    vmem = pl.BlockSpec(memory_space=pltpu.VMEM)
-    anyw = pl.BlockSpec(memory_space=pl.ANY)
+    hbm = pl.BlockSpec(memory_space=pltpu.HBM)
     dma = pltpu.SemaphoreType.DMA
-    return pl.pallas_call(
+    packed = pl.pallas_call(
         kernel,
-        out_shape=jax.ShapeDtypeStruct(state.shape, F32),
-        in_specs=[anyw, smem, smem, vmem, vmem, vmem, smem],
-        out_specs=anyw,
+        out_shape=jax.ShapeDtypeStruct(whole, F32),
+        in_specs=[hbm] * 7,
+        out_specs=hbm,
         scratch_shapes=[
             pltpu.VMEM((ROWS, LOCAL), F32),
-            pltpu.VMEM((ROWS, LOCAL), F32),
-            pltpu.VMEM(whole, F32),
-            pltpu.VMEM(whole, F32),
+            pltpu.SMEM((BLOCKS,), jnp.int32),
+            pltpu.SMEM((BLOCKS,), jnp.int32),
+            pltpu.VMEM((BLOCKS, OBS), jnp.int32),
+            pltpu.VMEM((BLOCKS, OBS), F32),
+            pltpu.VMEM((BLOCKS, OBS), F32),
+            pltpu.SMEM((BLOCKS, GX * GY * LOCAL // TILE), jnp.int32),
+            pltpu.VMEM((MEM, CHUNKS, 8, QUADS * TILE), F32),
             pltpu.VMEM(whole, F32),
             pltpu.VMEM(whole, F32),
             pltpu.VMEM(slab, F32),
@@ -284,18 +325,32 @@
             pltpu.VMEM((MEM,) + slab, F32),
             pltpu.VMEM((1 << BLOCKS, M, KDIM), BF16),
             pltpu.VMEM((1 << (BLOCKS - 1), M, KDIM), F32),
-            dma, dma,
+            dma, dma((6,)), dma((CHUNKS,)),
             dma((CHUNKS, MEM - 1)), dma((CHUNKS, MEM - 1)),
+            dma((MEM - 1,)), dma((MEM - 1,)),
             dma((CHUNKS, MEM - 1)), dma((CHUNKS, MEM - 1)),
             dma((GX - 1,)), dma((GX - 1,)),
             dma((GY - 1,)), dma((GY - 1,)),
             dma((MEM - 1,)), dma((MEM - 1,)),
         ],
         compiler_params=pltpu.CompilerParams(
-            collective_id=0, has_side_effects=True, vmem_limit_bytes=40 << 20
+            collective_id=0, has_side_effects=True, vmem_limit_bytes=64 << 20
         ),
         name="ensemble_update",
     )(state, obs_tile, block_order, obs_offset, obs_value, obs_error, loc_mask)
+    return pl.pallas_call(
+        unpack,
+        out_shape=jax.ShapeDtypeStruct(state.shape, F32),
+        in_specs=[hbm],
+        out_specs=hbm,
+        scratch_shapes=[
+            pltpu.VMEM(whole, F32),
+            pltpu.VMEM((ROWS - 8, LOCAL), F32),
+            dma((MEM,)), dma((MEM, CHUNKS)), dma((MEM,)),
+        ],
+        compiler_params=pltpu.CompilerParams(vmem_limit_bytes=64 << 20),
+        name="unpack",
+    )(packed)
 
 
 def solution(mesh):

time: 52.5 us -> 44.8 us (0.85)
  local copies, waits for them, and re-layouts: 7.12 us -> 0 us
    unnamed x15 -> x0, local copies, waits for them, and re-layouts: 7.12 us -> none
    pallas_call x1 -> x2, Pallas kernels: 45.1 us -> 44.6 us  [the longest x1 42.1 us: on_device(): pl.pallas_call(kernel, out_shape=jax.ShapeDtypeStruct(whole, F32), in_spe...]
where the time goes in v2:
time: 44.8 us; the launch traced here: 44.6 us
  Pallas kernels  44.6 us (100%)
    pallas_call x1, Pallas kernels, on_device(): pl.pallas_call(kernel, out_shape=jax.ShapeDtypeStruct(whole, F32), in_spe...  42.1 us
    pallas_call x1, Pallas kernels, on_device(): pl.pallas_call(unpack, out_shape=jax.ShapeDtypeStruct(state.shape, F32),...  2.48 us

profile of v2, /device:TPU:1, one launch (start us, length us, event | category | flops | bytes accessed | tf_op | source)
XLA Modules:
  0.0 44.6 jit_solution(3777823379360505279)
XLA Ops:
  0.0 42.1 %ensemble_update.1.packed = f32[8,4,8,1280]{3,2,1,0:T(8,128)} custom-call(f32[10,32768]{1,0:T(8,128)} %x_hbm.1, s32[4]{0:T(128)} %tile_hbm.1, s32[4]{0:T(128)} %order_hbm.1, s32[4,256]{1,0:T(4,128)} %off_hbm.1, f32[4,256]{1,0:T(4,128)} %val_hbm.1, f32[4,256]{1,0:T(4,128)} %err_hbm.1, s32[4,4096]{1,0:T(4,128)} %mask_hbm.1), custom_call_target="tpu_custom_call" | custom-call | tf_op jit(solution)/shard_map/ensemble_update/pallas_call | solution.py:304
  42.1 2.5 %unpack.1 = f32[10,32768]{1,0:T(8,128)} custom-call(f32[8,4,8,1280]{3,2,1,0:T(8,128)} %ensemble_update.1.packed), custom_call_target="tpu_custom_call" | custom-call | tf_op jit(solution)/shard_map/unpack/pallas_call | solution.py:341

commit v3 on v2

--- a/solution.py
+++ b/solution.py
@@ -16,12 +16,15 @@
 BLOCKS = 4
 TILE = 128
 QUAD = 4
-CHUNKS = 4
-QUADS = 2
+CHUNKS = 2
+QUADS = 4
 WIDTH = QUADS * QUAD * TILE
 OWN = CHUNKS * WIDTH
 LOCAL = MEM * OWN
 PACKED = WIDTH + QUADS * TILE
+DEPTH = 21
+LOADS = 4
+HOPS = [(1, 0), (3, 0), (2, 1), (1, 1), (3, 1), (2, 0), (0, 1)]
 KDIM = 256
 
 
@@ -90,7 +93,8 @@
             src_ref=src, dst_ref=dst, send_sem=s, recv_sem=r, device_id=peer, device_id_type=MESH
         )
 
-    mem_peers = [{"mem": lax.rem(me + k, MEM)} for k in range(1, MEM)]
+    z, core = me // 2, lax.rem(me, 2)
+    mem_peers = [{"mem": lax.rem(z + dz, MEM // 2) * 2 + lax.rem(core + dc, 2)} for dz, dc in HOPS]
     x_peers = [{"grid": lax.rem(gx + k, GX) * GY + gy} for k in range(1, GX)]
     y_peers = [{"grid": gx * GY + lax.rem(gy + k, GY)} for k in range(1, GY)]
     barrier = pltpu.get_barrier_semaphore()
@@ -104,9 +108,11 @@
             (off_hbm, off_ref), (val_hbm, val_ref), (err_hbm, err_ref),
         ])
     ]
-    load_x = pltpu.make_async_copy(x_hbm, x_v, x_sem)
-    load_x.start()
-    for c in small:
+    load_x = []
+    for i in range(LOADS):
+        cols = pl.ds(i * (LOCAL // LOADS), LOCAL // LOADS)
+        load_x.append(pltpu.make_async_copy(x_hbm.at[:, cols], x_v.at[:, cols], x_sem.at[i]))
+    for c in small[:2] + load_x + small[2:]:
         c.start()
 
     def columns(d, q):
@@ -122,13 +128,19 @@
         dst = recv1.at[me, :, :, WIDTH:PACKED]
         return remote(tails.at[peer["mem"]], dst, tsend.at[k], trecv.at[k], peer)
 
-    def push(q):
-        for k in range(MEM - 1):
-            out1(q, k).start()
-
-    for c in small:
-        c.wait()
-    load_x.wait()
+    pieces = [out1(q, k) for q in range(CHUNKS) for k in range(MEM - 1)]
+    pieces[7:7] = [out_tails(k) for k in range(MEM - 1)]
+
+    def feed(upto):
+        while fed[0] < upto:
+            if fed[0] >= DEPTH:
+                pieces[fed[0] - DEPTH].wait_send()
+            pieces[fed[0]].start()
+            fed[0] += 1
+
+    fed = [0]
+    for c in small[:2] + load_x:
+        c.wait()
 
     blocks = [order_ref[k] for k in range(BLOCKS)]
     tiles = [tile_ref[blocks[k]] for k in range(BLOCKS)]
@@ -146,7 +158,7 @@
     cx = [remote(slab_a, got_x.at[k], xs.at[k], xr.at[k], x_peers[k]) for k in range(GX - 1)]
     for c in cx:
         c.start()
-    push(0)
+    feed(7)
 
     def pack(d, c):
         for q in range(CHUNKS):
@@ -157,23 +169,6 @@
         return c
 
     lax.fori_loop(0, MEM, pack, 0)
-    for c in cx:
-        c.wait()
-    slab_b[...] = slab_a[...] + got_x[0] + got_x[1] + got_x[2]
-    cy = [remote(slab_b, got_y.at[k], ys.at[k], yr.at[k], y_peers[k]) for k in range(GY - 1)]
-    for c in cy:
-        c.start()
-    for k in range(MEM - 1):
-        out_tails(k).start()
-    for c in cy:
-        c.wait()
-    slab_c[...] = slab_b[...] + got_y[0] + got_y[1] + got_y[2]
-    cm = [remote(slab_c, got_m.at[me], ms.at[k], mr.at[k], mem_peers[k]) for k in range(MEM - 1)]
-    for c in cm:
-        c.start()
-    got_m[me] = slab_c[...]
-    for q in range(1, CHUNKS):
-        push(q)
     own = [
         pltpu.make_async_copy(x_hbm.at[0:8, columns(me, q)], recv1.at[me, q, :, 0:WIDTH], own_sem.at[q])
         for q in range(CHUNKS)
@@ -181,9 +176,27 @@
     for c in own:
         c.start()
     recv1[me, :, :, WIDTH:PACKED] = tails[me]
+    feed(7)
+    for c in cx:
+        c.wait()
+    slab_b[...] = slab_a[...] + got_x[0] + got_x[1] + got_x[2]
+    cy = [remote(slab_b, got_y.at[k], ys.at[k], yr.at[k], y_peers[k]) for k in range(GY - 1)]
+    for c in cy:
+        c.start()
+    feed(14)
+    for c in cy:
+        c.wait()
+    slab_c[...] = slab_b[...] + got_y[0] + got_y[1] + got_y[2]
+    cm = [remote(slab_c, got_m.at[me], ms.at[k], mr.at[k], mem_peers[k]) for k in range(MEM - 1)]
     for c in cm:
-        c.wait()
-
+        c.start()
+    got_m[me] = slab_c[...]
+    feed(21)
+    for c in cm:
+        c.wait()
+
+    for c in small[2:]:
+        c.wait()
     slabs = gathered_quad(lambda s, t: got_m[s, t], lambda s: got_m[s, QUAD])
     lane = lax.broadcasted_iota(jnp.int32, (M, KDIM), 1)
     row = lax.broadcasted_iota(jnp.int32, (M, KDIM), 0)
@@ -225,10 +238,11 @@
                 amat[(1 << k) + p] = new
             hc[(1 << k) + p] = left_form(new - eye)
 
+    feed(len(pieces))
     for c in own:
         c.wait()
     for k in range(MEM - 1):
-        out_tails(k).wait()
+        out_tails(k).wait_recv()
 
     def out2(q, k):
         peer = mem_peers[k]
@@ -241,7 +255,7 @@
 
     def update(q, c):
         for k in range(MEM - 1):
-            out1(q, k).wait()
+            out1(q, k).wait_recv()
         for u in range(QUADS):
             quad = gathered_quad(
                 lambda s, t: recv1[s, q, :, lanes(u * QUAD + t)], lambda s: recv1[s, q, :, lanes(QUADS * QUAD + u)]
@@ -271,24 +285,23 @@
         keep(q).wait()
         for k in range(MEM - 1):
             out2(q, k).wait()
-
-
-def unpack(packed, out, held, rows_v, in_sem, main_sem, row_sem):
-    loads = [pltpu.make_async_copy(packed.at[d], held.at[d], in_sem.at[d]) for d in range(MEM)]
-    for c in loads:
-        c.start()
+    for piece in pieces[-DEPTH:]:
+        piece.wait_send()
+
+
+def unpack(packed, out, rows_v, main_sem, row_sem):
     started = []
     for d in range(MEM):
-        loads[d].wait()
         for q in range(CHUNKS):
             cols = pl.ds(d * OWN + q * WIDTH, WIDTH)
-            started.append(pltpu.make_async_copy(held.at[d, q, :, 0:WIDTH], out.at[0:8, cols], main_sem.at[d, q]))
+            started.append(pltpu.make_async_copy(packed.at[d, q, :, 0:WIDTH], out.at[0:8, cols], main_sem.at[d, q]))
             started[-1].start()
+    for d in range(MEM):
         for q in range(CHUNKS):
             for u in range(QUADS):
                 for t in range(QUAD):
                     col = d * OWN + q * WIDTH + (u * QUAD + t) * TILE
-                    rows_v[:, col : col + TILE] = held[d, q, 2 * t : 2 * t + 2, WIDTH + u * TILE : WIDTH + (u + 1) * TILE]
+                    rows_v[:, col : col + TILE] = packed[d, q, 2 * t : 2 * t + 2, WIDTH + u * TILE : WIDTH + (u + 1) * TILE]
         cols = pl.ds(d * OWN, OWN)
         started.append(pltpu.make_async_copy(rows_v.at[:, cols], out.at[8:10, cols], row_sem.at[d]))
         started[-1].start()
@@ -301,6 +314,8 @@
     slab = (QUAD + 1, 8, TILE)
     hbm = pl.BlockSpec(memory_space=pltpu.HBM)
     dma = pltpu.SemaphoreType.DMA
+    args = (state, obs_tile, block_order, obs_offset, obs_value, obs_error, loc_mask)
+    args = [pltpu.with_memory_space_constraint(a, pltpu.HBM) for a in args]
     packed = pl.pallas_call(
         kernel,
         out_shape=jax.ShapeDtypeStruct(whole, F32),
@@ -325,7 +340,7 @@
             pltpu.VMEM((MEM,) + slab, F32),
             pltpu.VMEM((1 << BLOCKS, M, KDIM), BF16),
             pltpu.VMEM((1 << (BLOCKS - 1), M, KDIM), F32),
-            dma, dma((6,)), dma((CHUNKS,)),
+            dma((LOADS,)), dma((6,)), dma((CHUNKS,)),
             dma((CHUNKS, MEM - 1)), dma((CHUNKS, MEM - 1)),
             dma((MEM - 1,)), dma((MEM - 1,)),
             dma((CHUNKS, MEM - 1)), dma((CHUNKS, MEM - 1)),
@@ -334,21 +349,17 @@
             dma((MEM - 1,)), dma((MEM - 1,)),
         ],
         compiler_params=pltpu.CompilerParams(
-            collective_id=0, has_side_effects=True, vmem_limit_bytes=64 << 20
+            collective_id=0, has_side_effects=True, vmem_limit_bytes=40 << 20
         ),
         name="ensemble_update",
-    )(state, obs_tile, block_order, obs_offset, obs_value, obs_error, loc_mask)
+    )(*args)
     return pl.pallas_call(
         unpack,
         out_shape=jax.ShapeDtypeStruct(state.shape, F32),
-        in_specs=[hbm],
+        in_specs=[pl.BlockSpec(memory_space=pltpu.VMEM)],
         out_specs=hbm,
-        scratch_shapes=[
-            pltpu.VMEM(whole, F32),
-            pltpu.VMEM((ROWS - 8, LOCAL), F32),
-            dma((MEM,)), dma((MEM, CHUNKS)), dma((MEM,)),
-        ],
-        compiler_params=pltpu.CompilerParams(vmem_limit_bytes=64 << 20),
+        scratch_shapes=[pltpu.VMEM((ROWS - 8, LOCAL), F32), dma((MEM, CHUNKS)), dma((MEM,))],
+        compiler_params=pltpu.CompilerParams(vmem_limit_bytes=16 << 20),
         name="unpack",
     )(packed)
 

time: 44.8 us -> 42.4 us (0.946)
  Pallas kernels: 44.6 us -> 42.2 us
    pallas_call x1, Pallas kernels: 2.48 us -> 1.24 us  [on_device(): pl.pallas_call(unpack, out_shape=jax.ShapeDtypeStruct(state.shape, F32),...]
    pallas_call x1, Pallas kernels: 42.1 us -> 41 us  [on_device(): pl.pallas_call(kernel, out_shape=jax.ShapeDtypeStruct(whole, F32), in_spe...]
where the time goes in v3:
time: 42.4 us; the launch traced here: 42.2 us
  Pallas kernels  42.2 us (100%)
    pallas_call x1, Pallas kernels, on_device(): pl.pallas_call(kernel, out_shape=jax.ShapeDtypeStruct(whole, F32), in_spe...  41 us
    pallas_call x1, Pallas kernels, on_device(): pl.pallas_call(unpack, out_shape=jax.ShapeDtypeStruct(state.shape, F32),...  1.24 us

profile of v3, /device:TPU:1, one launch (start us, length us, event | category | flops | bytes accessed | tf_op | source)
XLA Modules:
  0.0 42.2 jit_solution(5605722160379319678)
XLA Ops:
  0.0 41.0 %ensemble_update.1.packed = f32[8,2,8,2560]{3,2,1,0:T(8,128)S(1)} custom-call(f32[10,32768]{1,0:T(8,128)} %x_hbm.1, s32[4]{0:T(128)} %tile_hbm.1, s32[4]{0:T(128)} %order_hbm.1, s32[4,256]{1,0:T(4,128)} %off_hbm.1, f32[4,256]{1,0:T(4,128)} %val_hbm.1, f32[4,256]{1,0:T(4,128)} %err_hbm.1, s32[4,4096]{1,0:T(4,128)} %mask_hbm.1), custom_call_target="tpu_custom_call" | custom-call | tf_op jit(solution)/shard_map/ensemble_update/pallas_call | solution.py:319
  41.0 1.2 %unpack.1 = f32[10,32768]{1,0:T(8,128)} custom-call(f32[8,2,8,2560]{3,2,1,0:T(8,128)S(1)} %ensemble_update.1.packed), custom_call_target="tpu_custom_call" | custom-call | tf_op jit(solution)/shard_map/unpack/pallas_call | solution.py:356

commit v4 on v3

--- a/solution.py
+++ b/solution.py
@@ -81,7 +81,7 @@
     x_hbm, tile_hbm, order_hbm, off_hbm, val_hbm, err_hbm, mask_hbm,
     recv2,
     x_v, tile_ref, order_ref, off_ref, val_ref, err_ref, mask_ref,
-    tails, recv1, send2, slab_a, slab_b, slab_c, got_x, got_y, got_m, hc, amat,
+    tails, recv1, send2, slab_a, slab_b, slab_c, got_x, got_y, got_m, hc,
     x_sem, in_sem, own_sem, ssem1, rsem1, tsend, trecv, ssem2, rsem2, xs, xr, ys, yr, ms, mr,
 ):
     me = lax.axis_index("mem")
@@ -158,7 +158,7 @@
     cx = [remote(slab_a, got_x.at[k], xs.at[k], xr.at[k], x_peers[k]) for k in range(GX - 1)]
     for c in cx:
         c.start()
-    feed(7)
+    feed(5)
 
     def pack(d, c):
         for q in range(CHUNKS):
@@ -176,14 +176,14 @@
     for c in own:
         c.start()
     recv1[me, :, :, WIDTH:PACKED] = tails[me]
-    feed(7)
+    feed(5)
     for c in cx:
         c.wait()
     slab_b[...] = slab_a[...] + got_x[0] + got_x[1] + got_x[2]
     cy = [remote(slab_b, got_y.at[k], ys.at[k], yr.at[k], y_peers[k]) for k in range(GY - 1)]
     for c in cy:
         c.start()
-    feed(14)
+    feed(9)
     for c in cy:
         c.wait()
     slab_c[...] = slab_b[...] + got_y[0] + got_y[1] + got_y[2]
@@ -198,23 +198,22 @@
     for c in small[2:]:
         c.wait()
     slabs = gathered_quad(lambda s, t: got_m[s, t], lambda s: got_m[s, QUAD])
-    lane = lax.broadcasted_iota(jnp.int32, (M, KDIM), 1)
-    row = lax.broadcasted_iota(jnp.int32, (M, KDIM), 0)
-    eye = jnp.where(lax.rem(lane, M) == row, 1.0, 0.0).astype(F32)
-    amat[0] = eye
-    hc[0] = jnp.zeros((M, KDIM), BF16)
+    sublane = lax.broadcasted_iota(jnp.int32, (TILE, OBS), 0)
+    priors = []
+    for k in range(BLOCKS):
+        hot = jnp.where(sublane == off_ref[pl.ds(blocks[k], 1), :], 1.0, 0.0).astype(BF16)
+        top, rest = split(slabs[k])
+        low = (slabs[k] - top.astype(F32) - rest.astype(F32)).astype(BF16)
+        priors.append(dot(top, hot) + (dot(rest, hot) + dot(low, hot)))
+    pad = jnp.zeros((KDIM - 3 * M, OBS), BF16)
+    none = jnp.zeros((M, KDIM), BF16)
+    last = None
     for k in range(BLOCKS):
         b = blocks[k]
-        off = off_ref[pl.ds(b, 1), :]
         val = val_ref[pl.ds(b, 1), :]
         err = err_ref[pl.ds(b, 1), :]
-        sublane = lax.broadcasted_iota(jnp.int32, (TILE, OBS), 0)
-        hot = jnp.where(sublane == off, 1.0, 0.0).astype(BF16)
-        top, rest = split(slabs[k])
-        low = (slabs[k] - top.astype(F32) - rest.astype(F32)).astype(BF16)
-        prior = dot(top, hot) + (dot(rest, hot) + dot(low, hot))
-        ybar = jnp.sum(prior, axis=0, keepdims=True) * (1.0 / M)
-        dev = prior - ybar
+        ybar = jnp.sum(priors[k], axis=0, keepdims=True) * (1.0 / M)
+        dev = priors[k] - ybar
         var = jnp.sum(dev * dev, axis=0, keepdims=True) * (1.0 / (M - 1.0))
         total = var + err
         lead = var / total * (val - ybar)
@@ -223,20 +222,21 @@
         weighted = dev * (1.0 / ((M - 1.0) * (var + 1e-05)))
         dh, dl = split(dy)
         wh, wl = split(weighted)
-        pad = jnp.zeros((KDIM - 3 * M, OBS), BF16)
         wh = jnp.concatenate([wh, wh, wh, pad], axis=0)
         wl = jnp.concatenate([wl, wl, wl, pad], axis=0)
         tri = dot_nt(dh, wh) + (dot_nt(dh, wl) + dot_nt(dl, wh))
         left = left_form(tri)
         for j in range(k + 1, BLOCKS):
             on = mask_ref[b, tiles[j]].astype(F32)
-            slabs[j] = slabs[j] + on * dot(left, stacked(slabs[j]))
-        for p in range(1 << k):
-            base = amat[p]
-            new = base + (tri if p == 0 else dot(left, stacked(base)))
-            if k < BLOCKS - 1:
-                amat[(1 << k) + p] = new
-            hc[(1 << k) + p] = left_form(new - eye)
+            priors[j] = priors[j] + on * dot(left, stacked(priors[j]))
+        at = 4 * (k // 2)
+        if k % 2 == 0:
+            hc[at] = none
+            hc[at + 1] = left
+            last = tri
+        else:
+            hc[at + 2] = left
+            hc[at + 3] = left_form(last + tri + dot(left, stacked(last)))
 
     feed(len(pieces))
     for c in own:
@@ -263,10 +263,10 @@
             pairs = [[], []]
             for t in range(QUAD):
                 tile = first_tile + q * (QUADS * QUAD) + (u * QUAD + t)
-                pattern = jnp.int32(0)
-                for k in range(BLOCKS):
-                    pattern = pattern + mask_ref[blocks[k], tile] * (1 << k)
-                y = quad[t] + dot(hc[pattern], stacked(quad[t]))
+                y = quad[t]
+                for h in range(2):
+                    on = [mask_ref[blocks[2 * h + k], tile] for k in range(2)]
+                    y = y + dot(hc[4 * h + on[0] + 2 * on[1]], stacked(y))
                 for d in range(MEM):
                     send2[d, q, :, lanes(u * QUAD + t)] = y[8 * d : 8 * d + 8]
                 for h in range(2):
@@ -338,8 +338,7 @@
             pltpu.VMEM((GX - 1,) + slab, F32),
             pltpu.VMEM((GY - 1,) + slab, F32),
             pltpu.VMEM((MEM,) + slab, F32),
-            pltpu.VMEM((1 << BLOCKS, M, KDIM), BF16),
-            pltpu.VMEM((1 << (BLOCKS - 1), M, KDIM), F32),
+            pltpu.VMEM((2 * BLOCKS, M, KDIM), BF16),
             dma((LOADS,)), dma((6,)), dma((CHUNKS,)),
             dma((CHUNKS, MEM - 1)), dma((CHUNKS, MEM - 1)),
             dma((MEM - 1,)), dma((MEM - 1,)),

time: 42.4 us -> 41.1 us (0.969)
  Pallas kernels: 42.2 us -> 40.9 us
    pallas_call x1, Pallas kernels: 41 us -> 39.7 us  [on_device(): pl.pallas_call(kernel, out_shape=jax.ShapeDtypeStruct(whole, F32), in_spe...]
where the time goes in v4:
time: 41.1 us; the launch traced here: 40.9 us
  Pallas kernels  40.9 us (100%)
    pallas_call x1, Pallas kernels, on_device(): pl.pallas_call(kernel, out_shape=jax.ShapeDtypeStruct(whole, F32), in_spe...  39.7 us
    pallas_call x1, Pallas kernels, on_device(): pl.pallas_call(unpack, out_shape=jax.ShapeDtypeStruct(state.shape, F32),...  1.24 us

profile of v4, /device:TPU:1, one launch (start us, length us, event | category | flops | bytes accessed | tf_op | source)
XLA Modules:
  0.0 40.9 jit_solution(12735124794106062273)
XLA Ops:
  0.0 39.7 %ensemble_update.1.packed = f32[8,2,8,2560]{3,2,1,0:T(8,128)S(1)} custom-call(f32[10,32768]{1,0:T(8,128)} %x_hbm.1, s32[4]{0:T(128)} %tile_hbm.1, s32[4]{0:T(128)} %order_hbm.1, s32[4,256]{1,0:T(4,128)} %off_hbm.1, f32[4,256]{1,0:T(4,128)} %val_hbm.1, f32[4,256]{1,0:T(4,128)} %err_hbm.1, s32[4,4096]{1,0:T(4,128)} %mask_hbm.1), custom_call_target="tpu_custom_call" | custom-call | tf_op jit(solution)/shard_map/ensemble_update/pallas_call | solution.py:319
  39.7 1.2 %unpack.1 = f32[10,32768]{1,0:T(8,128)} custom-call(f32[8,2,8,2560]{3,2,1,0:T(8,128)S(1)} %ensemble_update.1.packed), custom_call_target="tpu_custom_call" | custom-call | tf_op jit(solution)/shard_map/unpack/pallas_call | solution.py:355

commit v5 on v4

--- a/solution.py
+++ b/solution.py
@@ -139,6 +139,9 @@
             fed[0] += 1
 
     fed = [0]
+    pl.semaphore_wait(barrier, MEM - 1 + GX - 1 + GY - 1)
+
+    feed(3)
     for c in small[:2] + load_x:
         c.wait()
 
@@ -152,8 +155,6 @@
         mine = jnp.full((8, TILE), away, jnp.int32) == 0
         slab_a[k] = jnp.where(mine, x_v[0:8, pl.ds(start, TILE)], 0.0)
         slab_a[QUAD, 2 * k : 2 * k + 2, :] = jnp.where(mine[0:2], x_v[8:10, pl.ds(start, TILE)], 0.0)
-
-    pl.semaphore_wait(barrier, MEM - 1 + GX - 1 + GY - 1)
 
     cx = [remote(slab_a, got_x.at[k], xs.at[k], xr.at[k], x_peers[k]) for k in range(GX - 1)]
     for c in cx:

time: 41.1 us -> 41.1 us (level)
  no operation moved by 1% of the time
where the time goes in v5:
time: 41.1 us; the launch traced here: 41 us
  Pallas kernels  41 us (100%)
    pallas_call x1, Pallas kernels, on_device(): pl.pallas_call(kernel, out_shape=jax.ShapeDtypeStruct(whole, F32), in_spe...  39.7 us
    pallas_call x1, Pallas kernels, on_device(): pl.pallas_call(unpack, out_shape=jax.ShapeDtypeStruct(state.shape, F32),...  1.24 us

profile of v5, /device:TPU:1, one launch (start us, length us, event | category | flops | bytes accessed | tf_op | source)
XLA Modules:
  0.0 41.0 jit_solution(12938790267058581060)
XLA Ops:
  0.0 39.7 %ensemble_update.1.packed = f32[8,2,8,2560]{3,2,1,0:T(8,128)S(1)} custom-call(f32[10,32768]{1,0:T(8,128)} %x_hbm.1, s32[4]{0:T(128)} %tile_hbm.1, s32[4]{0:T(128)} %order_hbm.1, s32[4,256]{1,0:T(4,128)} %off_hbm.1, f32[4,256]{1,0:T(4,128)} %val_hbm.1, f32[4,256]{1,0:T(4,128)} %err_hbm.1, s32[4,4096]{1,0:T(4,128)} %mask_hbm.1), custom_call_target="tpu_custom_call" | custom-call | tf_op jit(solution)/shard_map/ensemble_update/pallas_call | solution.py:320
  39.7 1.2 %unpack.1 = f32[10,32768]{1,0:T(8,128)} custom-call(f32[8,2,8,2560]{3,2,1,0:T(8,128)S(1)} %ensemble_update.1.packed), custom_call_target="tpu_custom_call" | custom-call | tf_op jit(solution)/shard_map/unpack/pallas_call | solution.py:356
